TPU v7x, 128 devices: a whole 4x4x4 slice. The times are simulated.
128 devices in a mesh: pts: 8 (over x, core), shk: 16 (over z, y).
Axes of the slice: x: 4, y: 4, z: 4, core: 2. Of those that a mesh axis runs over, the one named last changes fastest.
Arguments:
- savings: float32 [16, 59, 1024], P('shk', None, 'pts'), may hold values from 0.05 to 0.95
- wealth: float32 [16, 59, 1024], P('shk', None, 'pts'), may hold values from 0.5 to 2
- surplus: bfloat16 [16, 118, 2048], P('shk', None, 'pts'), may hold values from -0.12 to 0.12
- point_dims: int32 [16, 3, 2048], P('shk', None, 'pts'), may hold values from 0 to 58
- point_levels: int32 [16, 3, 2048], P('shk', None, 'pts'), may hold values from 0 to 3
- point_index: int32 [16, 3, 2048], P('shk', None, 'pts'), may hold values from 1 to 7, as said below
- live_count: int32 [16, 8], P('shk', 'pts'), may hold values from 64 to 256
- trans_counts: int32 [16, 16], replicated, may hold values from 1 to 99
Outputs:
- savings_out: float32 [16, 59, 1024], P('shk', None, 'pts')
- consumption: float32 [16, 59, 1024], P('shk', None, 'pts')
Inputs may be any that keep to these rules, and one draw needn't show every extreme that they name: `point_index`: odd, below 2 ** level where the level is positive, 1 where it is 0. Points at positions from live_count on in a shard are padding.
All inputs are finite; a program needn't handle non-finite values.
Results may differ from a plain program's by a relative error of at most 0.0011.
Values may be sent and summed in bfloat16 or wider, within the bound.
No kernel may reach another device: no remote copies, remote signals or barrier semaphores. Data moves between devices by JAX's collectives and lax.ppermute only.
A program may use at most 192 MiB of HBM per device.

v0:
```python
import jax
import jax.numpy as jnp
from jax import lax
from jax.sharding import PartitionSpec as P

ITERS = 2
GAMMA = 2.0
BETA = 0.96
damping = 0.5
query_block = 2048


def hat_tables(levels, indices):
    scaled = jnp.exp2(levels.astype(jnp.float32))
    inverse = jnp.where(levels > 0, scaled, jnp.zeros_like(scaled))
    centre = indices.astype(jnp.float32) / scaled
    return (centre, inverse)


def basis_block(coords, dims, centre, inverse):
    chosen = jnp.take(coords, dims, axis=0)
    factor = jnp.maximum(0.0, 1.0 - jnp.abs(chosen - centre[:, :, None]) * inverse[:, :, None])
    product = factor[0]
    for slot in range(1, factor.shape[0]):
        product = product * factor[slot]
    return product.astype(jnp.bfloat16)


def make_evaluate(weights, dims, centre, inverse):

    def block_eval(coords):
        basis = basis_block(coords, dims, centre, inverse)
        return jnp.dot(weights, basis, preferred_element_type=jnp.float32)

    def evaluate(piece, start):
        coords = piece.astype(jnp.float32)
        breadth = coords.shape[1]
        stacked = coords.reshape(coords.shape[0], breadth // query_block, query_block).transpose(
            1, 0, 2
        )
        results = lax.map(block_eval, stacked)
        return results.transpose(1, 0, 2).reshape(results.shape[1], breadth)

    return evaluate


def per_device(
    savings, wealth, surplus, point_dims, point_levels, point_index, live_count, trans_counts
):
    npoints = surplus.shape[2]
    live = live_count[0, 0]
    position = lax.iota(jnp.int32, npoints)
    live_surplus = jnp.where(position[None, :] < live, surplus[0], jnp.zeros_like(surplus[0]))
    counts = trans_counts.astype(jnp.float32)
    prob = counts / jnp.sum(counts, axis=1, keepdims=True)
    shock = lax.axis_index("shk")
    shk_count = lax.axis_size("shk")
    current = savings[0]
    income = wealth[0]
    dimension = current.shape[0]
    nquery = current.shape[1]
    centre, inverse = hat_tables(point_levels[0], point_index[0])
    evaluate = make_evaluate(live_surplus, point_dims[0], centre, inverse)
    consumption = current
    for sweep in range(ITERS):
        query = current.astype(jnp.bfloat16)
        partial_value = evaluate(
            lax.all_gather(query, ("pts", "shk"), axis=1, tiled=True), jnp.int32(0)
        )
        mine = lax.psum_scatter(partial_value, "pts", scatter_dimension=1, tiled=True)
        marginal = jnp.exp(-GAMMA * mine[:dimension] + mine[dimension:]).reshape(
            dimension, shk_count, nquery
        )
        column = lax.dynamic_index_in_dim(prob, shock, 1, keepdims=False)
        terms = marginal * column[None, :, None]
        expect = lax.psum_scatter(terms, "shk", scatter_dimension=1, tiled=True)[:, 0, :]
        consumption = (BETA * expect) ** (-1.0 / GAMMA)
        current = (1.0 - damping) * current + damping * jax.nn.sigmoid(income - consumption)
    return (current[None], consumption[None])


def solution(mesh):
    return jax.shard_map(
        per_device,
        mesh=mesh,
        in_specs=(
            P("shk", None, "pts"),
            P("shk", None, "pts"),
            P("shk", None, "pts"),
            P("shk", None, "pts"),
            P("shk", None, "pts"),
            P("shk", None, "pts"),
            P("shk", "pts"),
            P(),
        ),
        out_specs=(P("shk", None, "pts"), P("shk", None, "pts")),
        check_vma=False,
    )
```

profile of v0, /device:TPU:0, one launch (start us, length us, event | category | flops | bytes accessed | tf_op | source)
XLA Modules:
  0.0 647.1 jit_solution(12382082039239027195)
XLA Ops:
  11.5 66.2 %all-gather.3.cloned.1.call-done = bf16[59,16384]{1,0:T(8,128)(2,1)} async-done(((bf16[59,128]{1,0:T(8,128)(2,1)}), bf16[59,16384]{1,0:T(8,128)(2,1)}) %all-gather.3.cloned.1.call-update) | async-done | bytes 1933328 | tf_op jit(solution)/shard_map/all_gather | solution.py:68
  77.7 1.9 transpose.41
  79.6 2.5 copy.39
  82.6 4.2 copy.73
  86.8 4.0 broadcast.101.clone
  90.8 90.0 %while.20 = (s32[]{:T(128)}, f32[8,118,2048]{2,1,0:T(8,128)}, f32[8,59,2048]{2,1,0:T(8,128)}, s32[3,256]{1,0:T(4,128)S(1)}, f32[3,256]{1,0:T(4,128)S(1)}, /*inde...) while((s32[]{:T(128)}, f32[8,118,2048]{2,1,0:T(8,128)}, f32[8,59,2048]{2,1,0:T(8,128)}, ...), condition=%wide.region_1.3_spmd, body=%wide.region_0.0_spmd.sunk | while | flops 134749952 | bytes 33501272 | solution.py:41
  91.9 5.0 gather_fusion
  97.0 3.6 fusion.49
  103.1 5.0 gather_fusion
  108.1 3.6 fusion.49
  111.7 1.5 fusion.50
  114.3 5.0 gather_fusion
  119.4 3.6 fusion.49
  123.0 1.4 fusion.50
  125.5 5.0 gather_fusion
  130.6 3.6 fusion.49
  134.2 1.4 fusion.50
  136.7 5.0 gather_fusion
  141.7 3.6 fusion.49
  145.4 1.4 fusion.50
  147.9 5.0 gather_fusion
  152.9 3.6 fusion.49
  156.5 1.4 fusion.50
  159.1 5.0 gather_fusion
  164.1 3.6 fusion.49
  167.7 1.4 fusion.50
  170.3 5.0 gather_fusion
  175.3 3.6 fusion.49
  180.8 7.7 %copy.26 = f32[118,8,2048]{2,1,0:T(8,128)S(1)} copy(f32[118,8,2048]{2,0,1:T(8,128)} %bitcast.15) | data formatting | bytes 15466496 | tf_op jit(solution)/shard_map/transpose | solution.py:42
  189.5 9.0 %copy.40 = f32[15,8,8,2048]{3,1,2,0:T(8,128)} copy(f32[15,8,8,2048]{3,2,1,0:T(8,128)S(1)} %bitcast.133) | data formatting | bytes 15728640
  199.5 48.4 %reduce-scatter.9.cloned.1.call-done = f32[118,2048]{1,0:T(8,128)} async-done(((f32[118,16384]{1,0:T(8,128)}), f32[118,2048]{1,0:T(8,128)}) %reduce-scatter.9.cloned.1.call-update) | async-done | bytes 966672 | tf_op jit(solution)/shard_map/reduce_scatter | solution.py:70
  250.5 74.0 %reduce-scatter.13.cloned.1.call-done = f32[59,1,128]{2,0,1:T(8,128)} async-done(((f32[59,16,128]{2,0,1:T(8,128)}), f32[59,1,128]{2,0,1:T(8,128)}) %reduce-scatter.13.cloned.1.call-update) | async-done | bytes 30224
  325.9 64.9 %all-gather.5.cloned.1.call-done = bf16[59,16384]{1,0:T(8,128)(2,1)} async-done(((bf16[59,128]{1,0:T(8,128)(2,1)}), bf16[59,16384]{1,0:T(8,128)(2,1)}) %all-gather.5.cloned.1.call-update) | async-done | bytes 1933328 | tf_op jit(solution)/shard_map/all_gather | solution.py:68
  390.8 1.9 transpose.42
  392.6 2.5 copy.42
  395.6 4.2 copy.72
  399.8 4.0 broadcast.101
  403.9 89.7 %while.21 = (s32[]{:T(128)}, f32[8,118,2048]{2,1,0:T(8,128)}, f32[8,59,2048]{2,1,0:T(8,128)}, s32[3,256]{1,0:T(4,128)S(1)}, f32[3,256]{1,0:T(4,128)S(1)}, /*inde...) while((s32[]{:T(128)}, f32[8,118,2048]{2,1,0:T(8,128)}, f32[8,59,2048]{2,1,0:T(8,128)}, ...), condition=%wide.region_6.8_spmd, body=%wide.region_5.7_spmd.sunk | while | flops 134749952 | bytes 33501272 | solution.py:41
  405.0 5.0 gather_fusion.1
  410.0 3.6 fusion.53
  416.1 5.0 gather_fusion.1
  421.2 3.6 fusion.53
  424.8 1.5 fusion.54
  427.4 5.0 gather_fusion.1
  432.4 3.6 fusion.53
  436.0 1.4 fusion.54
  438.6 5.0 gather_fusion.1
  443.6 3.6 fusion.53
  447.2 1.4 fusion.54
  449.8 5.0 gather_fusion.1
  454.8 3.6 fusion.53
  458.4 1.4 fusion.54
  460.9 5.0 gather_fusion.1
  466.0 3.6 fusion.53
  469.6 1.4 fusion.54
  472.1 5.0 gather_fusion.1
  477.2 3.6 fusion.53
  480.8 1.4 fusion.54
  483.3 5.0 gather_fusion.1
  488.4 3.6 fusion.53
  493.6 7.7 %copy.31 = f32[118,8,2048]{2,1,0:T(8,128)S(1)} copy(f32[118,8,2048]{2,0,1:T(8,128)} %bitcast.19) | data formatting | bytes 15466496 | tf_op jit(solution)/shard_map/transpose | solution.py:42
  502.3 9.0 %copy.43 = f32[15,8,8,2048]{3,1,2,0:T(8,128)} copy(f32[15,8,8,2048]{3,2,1,0:T(8,128)S(1)} %bitcast.132) | data formatting | bytes 15728640
  511.4 49.4 %reduce-scatter.11.cloned.1.call-done = f32[118,2048]{1,0:T(8,128)} async-done(((f32[118,16384]{1,0:T(8,128)}), f32[118,2048]{1,0:T(8,128)}) %reduce-scatter.11.cloned.1.call-update) | async-done | bytes 966672 | tf_op jit(solution)/shard_map/reduce_scatter | solution.py:70
  563.2 73.9 %reduce-scatter.15.cloned.1.call-done = f32[59,1,128]{2,0,1:T(8,128)} async-done(((f32[59,16,128]{2,0,1:T(8,128)}), f32[59,1,128]{2,0,1:T(8,128)}) %reduce-scatter.15.cloned.1.call-update) | async-done | bytes 30224
  (129 shorter events, 40.1 us)
Async XLA Ops:
  7.2 70.6 %all-gather.3.cloned.1.call-start = ((), (), s32[]{:S(2)}) async-start(), calls=%async_computation.4 | async-start | bytes 2113536 | tf_op jit(solution)/shard_map/all_gather | solution.py:68
  8.6 239.4 %reduce-scatter.9.cloned.1.call-start = ((), (), s32[]{:S(2)}) async-start(), calls=%async_computation.5 | async-start | bytes 8847360 | tf_op jit(solution)/shard_map/reduce_scatter | solution.py:70
  198.5 0.7 copy-start.3
  198.5 125.9 %copy-start = (f32[1,59,128]{2,0,1:T(1,128)S(1)}, f32[1,59,128]{2,0,1:T(1,128)}, u32[]{:S(2)}) copy-start(f32[1,59,128]{2,0,1:T(1,128)} %param.14) | copy-start | bytes 90628
  198.5 125.9 %copy-start.2 = (f32[1,59,128]{2,0,1:T(1,128)S(1)}, f32[1,59,128]{2,0,1:T(1,128)}, u32[]{:S(2)}) copy-start(f32[1,59,128]{2,0,1:T(1,128)} %param.15) | copy-start | bytes 90628
  198.5 125.9 %reduce-scatter.13.cloned.1.call-start = ((), (), s32[]{:S(2)}) async-start(), calls=%async_computation.8 | async-start | bytes 557056
  250.4 140.4 %all-gather.5.cloned.1.call-start = ((), (), s32[]{:S(2)}) async-start(), calls=%async_computation.6 | async-start | bytes 2113536 | tf_op jit(solution)/shard_map/all_gather | solution.py:68
  325.9 234.9 %reduce-scatter.11.cloned.1.call-start = ((), (), s32[]{:S(2)}) async-start(), calls=%async_computation.7 | async-start | bytes 8847360 | tf_op jit(solution)/shard_map/reduce_scatter | solution.py:70
  511.3 125.9 %copy-start.1 = (f32[59,1,128]{2,0,1:T(8,128)S(1)}, f32[59,1,128]{2,0,1:T(8,128)}, u32[]{:S(2)}) copy-start(f32[59,1,128]{2,0,1:T(8,128)} %reduce-scatter.13.cloned.1.call-done) | copy-start | bytes 90628
  511.3 125.8 %reduce-scatter.15.cloned.1.call-start = ((), (), s32[]{:S(2)}) async-start(), calls=%async_computation.9 | async-start | bytes 557056
Sparse Core Ops, SparseCore 0:
  11.3 66.3 all-gather.2
  198.7 49.2 reduce-scatter.8
  251.1 73.2 reduce-scatter.12
  327.7 63.0 all-gather.4
  511.5 49.2 reduce-scatter.10
  563.8 73.3 reduce-scatter.14
where the time goes:
time: 655 us; the launch traced here: 647 us
  waiting for transfers between devices  377 us (58%)
  local copies, waits for them, and re-layouts  160 us (24%)
  other arithmetic  71.1 us (11%)
  matrix products  22.8 us (3%)
  between operations  15.1 us (2%)
    unnamed x8, waiting for transfers between devices  148 us
    all_gather x2, waiting for transfers between devices, per_device(): lax.all_gather(query, ('pts', 'shk'), axis=1, tiled=True)  131 us
    reduce_scatter x2, waiting for transfers between devices, per_device(): lax.psum_scatter(partial_value, 'pts', scatter_dimension=1, tiled=True)  97.8 us
    gather x16, local copies, waits for them, and re-layouts, basis_block(): chosen = jnp.take(coords, dims, axis=0)  80.3 us
    max x16, other arithmetic, basis_block(): jnp.maximum(0.0, 1.0 - jnp.abs(chosen - centre[:, :, None]) * inverse[:,...  57.7 us
    unnamed x20, local copies, waits for them, and re-layouts  29 us
    dot_general x16, matrix products, block_eval(): return jnp.dot(weights, basis, preferred_element_type=jnp.float32)  22.8 us
    squeeze x16, local copies, waits for them, and re-layouts, evaluate(): results = lax.map(block_eval, stacked)  17.2 us
  transfers between devices with their start and end apart: 6, of which 6 were waited for; matrix products, arithmetic and copies ran while one was open for 0% of the time, Pallas kernels for 0%

commit v1 on v0

--- a/solution.py
+++ b/solution.py
@@ -64,9 +64,17 @@
     consumption = current
     for sweep in range(ITERS):
         query = current.astype(jnp.bfloat16)
-        partial_value = evaluate(
-            lax.all_gather(query, ("pts", "shk"), axis=1, tiled=True), jnp.int32(0)
-        )
+
+        def answer_the_plate(m):
+            windows = []
+            for _ in range(lax.axis_size(("pts", "shk"))):
+                windows.append(m)
+            d_next = jnp.concatenate(
+                lax.all_to_all(jnp.stack(windows, axis=0), ("pts", "shk"), 0, 0), axis=1
+            )
+            return d_next
+
+        partial_value = evaluate(answer_the_plate(query), jnp.int32(0))
         mine = lax.psum_scatter(partial_value, "pts", scatter_dimension=1, tiled=True)
         marginal = jnp.exp(-GAMMA * mine[:dimension] + mine[dimension:]).reshape(
             dimension, shk_count, nquery

time: 655 us -> 618 us (0.944)
  waiting for transfers between devices: 377 us -> 268 us
  blocking collectives: 0 us -> 37.5 us
  local copies, waits for them, and re-layouts: 160 us -> 189 us
  starting transfers between devices: 0.42 us -> 11.5 us
    all_gather x2 -> x0, waiting for transfers between devices: 131 us -> none  [per_device(): lax.all_gather(query, ('pts', 'shk'), axis=1, tiled=True)]
    dynamic_slice x0 -> x32, local copies, waits for them, and re-layouts: none -> 42.4 us  [evaluate(): results = lax.map(block_eval, stacked)]
    all_to_all x0 -> x1, blocking collectives: none -> 37.5 us  [answer_the_plate(): lax.all_to_all(jnp.stack(windows, axis=0), ('pts', 'shk'), 0, 0)]
    all_to_all x0 -> x1, waiting for transfers between devices: none -> 29 us  [answer_the_plate(): lax.all_to_all(jnp.stack(windows, axis=0), ('pts', 'shk'), 0, 0)]
    squeeze x16 -> x0, local copies, waits for them, and re-layouts: 17.2 us -> none  [evaluate(): results = lax.map(block_eval, stacked)]
    all_to_all x0 -> x1, starting transfers between devices: none -> 11.2 us  [answer_the_plate(): lax.all_to_all(jnp.stack(windows, axis=0), ('pts', 'shk'), 0, 0)]
    transpose x4, local copies, waits for them, and re-layouts: 9.3 us -> 17.7 us  [evaluate(): coords.reshape(coords.shape[0], breadth // query_block, query_block)]
    unnamed x20 -> x26, local copies, waits for them, and re-layouts: 29 us -> 22 us
  transfers between devices with their start and end apart: 6 -> 5, of which waited for: 6 -> 5; matrix products, arithmetic and copies ran while one was open for 0% -> 0% of each run, Pallas kernels for 0% -> 0%
where the time goes in v1:
time: 618 us; the launch traced here: 611 us
  waiting for transfers between devices  268 us (43%)
  local copies, waits for them, and re-layouts  189 us (31%)
  other arithmetic  67 us (11%)
  blocking collectives  37.5 us (6%)
  matrix products  23 us (4%)
  between operations  14.9 us (2%)
  starting transfers between devices  11.5 us (2%)
    unnamed x6, waiting for transfers between devices  148 us
    reduce_scatter x2, waiting for transfers between devices, per_device(): lax.psum_scatter(partial_value, 'pts', scatter_dimension=1, tiled=True)  90.8 us
    gather x16, local copies, waits for them, and re-layouts, basis_block(): chosen = jnp.take(coords, dims, axis=0)  80.3 us
    max x16, other arithmetic, basis_block(): jnp.maximum(0.0, 1.0 - jnp.abs(chosen - centre[:, :, None]) * inverse[:,...  57.7 us
    dynamic_slice x32, local copies, waits for them, and re-layouts, evaluate(): results = lax.map(block_eval, stacked)  42.4 us
    all_to_all x1, blocking collectives, answer_the_plate(): lax.all_to_all(jnp.stack(windows, axis=0), ('pts', 'shk'), 0, 0)  37.5 us
    all_to_all x1, waiting for transfers between devices, answer_the_plate(): lax.all_to_all(jnp.stack(windows, axis=0), ('pts', 'shk'), 0, 0)  29 us
    dot_general x16, matrix products, block_eval(): return jnp.dot(weights, basis, preferred_element_type=jnp.float32)  23 us
  transfers between devices with their start and end apart: 5, of which 5 were waited for; matrix products, arithmetic and copies ran while one was open for 0% of the time, Pallas kernels for 0%

profile of v1, /device:TPU:0, one launch (start us, length us, event | category | flops | bytes accessed | tf_op | source)
XLA Modules:
  0.0 611.4 jit_solution(8692054768825686446)
XLA Ops:
  9.9 11.2 %all-to-all-start = ((bf16[128,59,128]{2,1,0:T(8,128)(2,1)}), bf16[128,59,128]{2,1,0:T(8,128)(2,1)S(1)}, u32[]{:S(2)}, u32[]{:S(2)}) async-start(bf16[128,59,128]{2,1,0:T(8,128)(2,1)} %stack.9), calls=%async_computation | async-start | bytes 4194304 | tf_op jit(solution)/shard_map/all_to_all | solution.py:73
  21.9 29.0 %all-to-all-done = bf16[128,59,128]{2,1,0:T(8,128)(2,1)S(1)} async-done(((bf16[128,59,128]{2,1,0:T(8,128)(2,1)}), bf16[128,59,128]{2,1,0:T(8,128)(2,1)S(1)}, u32[]{:S(2)}, u32[]{:S(2)}) %all-to-all-start) | async-done | bytes 1933344 | tf_op jit(solution)/shard_map/all_to_all | solution.py:73
  51.3 4.1 copy.20
  55.4 4.8 reshape.103
  60.2 4.0 broadcast.100.clone
  64.2 102.7 %while.20 = (s32[]{:T(128)}, f32[8,118,2048]{2,1,0:T(8,128)}, f32[8,59,2048]{2,0,1:T(8,128)}, s32[3,256]{1,0:T(4,128)S(1)}, f32[3,256]{1,0:T(4,128)S(1)}, /*inde...) while((s32[]{:T(128)}, f32[8,118,2048]{2,1,0:T(8,128)}, f32[8,59,2048]{2,0,1:T(8,128)}, ...), condition=%wide.region_1.3_spmd, body=%wide.region_0.0_spmd.sunk | while | flops 134749952 | bytes 34467928 | solution.py:41
  64.2 2.5 constant_dynamic-slice_fusion.4
  66.9 5.0 gather_fusion
  72.0 3.6 fusion.41
  77.0 2.5 constant_dynamic-slice_fusion.4
  79.7 5.0 gather_fusion
  84.7 3.6 fusion.41
  89.8 2.5 constant_dynamic-slice_fusion.4
  92.5 5.0 gather_fusion
  97.6 3.6 fusion.41
  102.6 2.5 constant_dynamic-slice_fusion.4
  105.3 5.0 gather_fusion
  110.3 3.6 fusion.41
  115.4 2.5 constant_dynamic-slice_fusion.4
  118.1 5.0 gather_fusion
  123.1 3.6 fusion.41
  128.2 2.5 constant_dynamic-slice_fusion.4
  130.9 5.0 gather_fusion
  135.9 3.6 fusion.41
  140.9 2.5 constant_dynamic-slice_fusion.4
  143.6 5.0 gather_fusion
  148.7 3.6 fusion.41
  153.7 2.5 constant_dynamic-slice_fusion.4
  156.4 5.0 gather_fusion
  161.5 3.6 fusion.41
  166.9 7.7 %copy.25 = f32[118,8,2048]{2,1,0:T(8,128)S(1)} copy(f32[118,8,2048]{2,0,1:T(8,128)} %bitcast.113) | data formatting | bytes 15466496 | tf_op jit(solution)/shard_map/transpose | solution.py:42
  175.7 9.0 %copy.40 = f32[15,8,8,2048]{3,1,2,0:T(8,128)} copy(f32[15,8,8,2048]{3,2,1,0:T(8,128)S(1)} %bitcast.110) | data formatting | bytes 15728640
  185.7 44.9 %reduce-scatter.9.cloned.1.call-done = f32[118,2048]{1,0:T(8,128)} async-done(((f32[118,16384]{1,0:T(8,128)}), f32[118,2048]{1,0:T(8,128)}) %reduce-scatter.9.cloned.1.call-update) | async-done | bytes 966672 | tf_op jit(solution)/shard_map/reduce_scatter | solution.py:78
  233.1 74.0 %reduce-scatter.13.cloned.1.call-done = f32[59,1,128]{2,0,1:T(8,128)} async-done(((f32[59,16,128]{2,0,1:T(8,128)}), f32[59,1,128]{2,0,1:T(8,128)}) %reduce-scatter.13.cloned.1.call-update) | async-done | bytes 30224
  308.4 37.5 %all_to_all.10 = bf16[128,59,128]{2,1,0:T(8,128)(2,1)S(1)} all-to-all(bf16[128,59,128]{2,1,0:T(8,128)(2,1)S(1)} %stack.11), channel_id=1, replica_groups=mesh['pts'=8,'shk'=16] {'pts','shk'}, dimensions={0} | all-to-all | bytes 3866624 | tf_op jit(solution)/shard_map/all_to_all | solution.py:73
  346.4 4.1 copy.29
  350.5 4.8 reshape.104
  355.3 4.0 broadcast.100
  359.3 102.4 %while.21 = (s32[]{:T(128)}, f32[8,118,2048]{2,1,0:T(8,128)}, f32[8,59,2048]{2,0,1:T(8,128)}, s32[3,256]{1,0:T(4,128)S(1)}, f32[3,256]{1,0:T(4,128)S(1)}, /*inde...) while((s32[]{:T(128)}, f32[8,118,2048]{2,1,0:T(8,128)}, f32[8,59,2048]{2,0,1:T(8,128)}, ...), condition=%wide.region_6.8_spmd, body=%wide.region_5.7_spmd.sunk | while | flops 134749952 | bytes 34467928 | solution.py:41
  359.3 2.5 constant_dynamic-slice_fusion.5
  362.0 5.0 gather_fusion.1
  367.0 3.6 fusion.45
  372.1 2.5 constant_dynamic-slice_fusion.5
  374.8 5.0 gather_fusion.1
  379.8 3.6 fusion.45
  384.9 2.5 constant_dynamic-slice_fusion.5
  387.6 5.0 gather_fusion.1
  392.6 3.6 fusion.45
  397.7 2.5 constant_dynamic-slice_fusion.5
  400.4 5.0 gather_fusion.1
  405.4 3.6 fusion.45
  410.5 2.5 constant_dynamic-slice_fusion.5
  413.2 5.0 gather_fusion.1
  418.2 3.6 fusion.45
  425.9 5.0 gather_fusion.1
  431.0 3.6 fusion.45
  438.7 5.0 gather_fusion.1
  443.7 3.6 fusion.45
  451.5 5.0 gather_fusion.1
  456.5 3.6 fusion.45
  461.8 7.7 %copy.31 = f32[118,8,2048]{2,1,0:T(8,128)S(1)} copy(f32[118,8,2048]{2,0,1:T(8,128)} %bitcast.114) | data formatting | bytes 15466496 | tf_op jit(solution)/shard_map/transpose | solution.py:42
  470.5 9.0 %copy.42 = f32[15,8,8,2048]{3,1,2,0:T(8,128)} copy(f32[15,8,8,2048]{3,2,1,0:T(8,128)S(1)} %bitcast.109) | data formatting | bytes 15728640
  479.6 45.8 %reduce-scatter.11.cloned.1.call-done = f32[118,2048]{1,0:T(8,128)} async-done(((f32[118,16384]{1,0:T(8,128)}), f32[118,2048]{1,0:T(8,128)}) %reduce-scatter.11.cloned.1.call-update) | async-done | bytes 966672 | tf_op jit(solution)/shard_map/reduce_scatter | solution.py:78
  527.9 73.9 %reduce-scatter.15.cloned.1.call-done = f32[59,1,128]{2,0,1:T(8,128)} async-done(((f32[59,16,128]{2,0,1:T(8,128)}), f32[59,1,128]{2,0,1:T(8,128)}) %reduce-scatter.15.cloned.1.call-update) | async-done | bytes 30224
  (151 shorter events, 49.1 us)
Async XLA Ops:
  7.2 14.6 %copy-start.5 = (s32[1,3,256]{2,0,1:T(1,128)S(1)}, s32[1,3,256]{2,0,1:T(1,128)}, u32[]{:S(2)}) copy-start(s32[1,3,256]{2,0,1:T(1,128)} %param.17) | copy-start | bytes 9220
  7.2 14.6 %copy-start.6 = (s32[1,3,256]{2,0,1:T(1,128)S(1)}, s32[1,3,256]{2,0,1:T(1,128)}, u32[]{:S(2)}) copy-start(s32[1,3,256]{2,0,1:T(1,128)} %param.18) | copy-start | bytes 9220
  7.2 14.6 %copy-start.7 = (s32[1,3,256]{2,0,1:T(1,128)S(1)}, s32[1,3,256]{2,0,1:T(1,128)}, u32[]{:S(2)}) copy-start(s32[1,3,256]{2,0,1:T(1,128)} %param.19) | copy-start | bytes 9220
  7.2 14.7 %copy-start.3 = (bf16[1,118,256]{2,1,0:T(8,128)(2,1)S(1)}, bf16[1,118,256]{2,1,0:T(8,128)(2,1)}, u32[]{:S(2)}) copy-start(bf16[1,118,256]{2,1,0:T(8,128)(2,1)} %param.16) | copy-start | bytes 181252
  9.9 41.0 %all-to-all-start = ((bf16[128,59,128]{2,1,0:T(8,128)(2,1)}), bf16[128,59,128]{2,1,0:T(8,128)(2,1)S(1)}, u32[]{:S(2)}, u32[]{:S(2)}) async-start(bf16[128,59,128]{2,1,0:T(8,128)(2,1)} %stack.9), calls=%async_computation | async-start | bytes 4194304 | tf_op jit(solution)/shard_map/all_to_all | solution.py:73
  21.1 209.5 %reduce-scatter.9.cloned.1.call-start = ((), (), s32[]{:S(2)}) async-start(), calls=%async_computation.6 | async-start | bytes 8847360 | tf_op jit(solution)/shard_map/reduce_scatter | solution.py:78
  184.7 0.7 copy-start.4
  184.7 122.4 %copy-start = (f32[1,59,128]{2,0,1:T(1,128)S(1)}, f32[1,59,128]{2,0,1:T(1,128)}, u32[]{:S(2)}) copy-start(f32[1,59,128]{2,0,1:T(1,128)} %param.14) | copy-start | bytes 90628
  184.7 122.4 %copy-start.2 = (f32[1,59,128]{2,0,1:T(1,128)S(1)}, f32[1,59,128]{2,0,1:T(1,128)}, u32[]{:S(2)}) copy-start(f32[1,59,128]{2,0,1:T(1,128)} %param.15) | copy-start | bytes 90628
  184.7 122.4 %reduce-scatter.13.cloned.1.call-start = ((), (), s32[]{:S(2)}) async-start(), calls=%async_computation.8 | async-start | bytes 557056
  233.1 292.4 %reduce-scatter.11.cloned.1.call-start = ((), (), s32[]{:S(2)}) async-start(), calls=%async_computation.7 | async-start | bytes 8847360 | tf_op jit(solution)/shard_map/reduce_scatter | solution.py:78
  479.5 122.3 %copy-start.1 = (f32[59,1,128]{2,0,1:T(8,128)S(1)}, f32[59,1,128]{2,0,1:T(8,128)}, u32[]{:S(2)}) copy-start(f32[59,1,128]{2,0,1:T(8,128)} %reduce-scatter.13.cloned.1.call-done) | copy-start | bytes 90628
  479.5 122.3 %reduce-scatter.15.cloned.1.call-start = ((), (), s32[]{:S(2)}) async-start(), calls=%async_computation.9 | async-start | bytes 557056
Sparse Core Ops, SparseCore 0:
  184.8 45.7 reduce-scatter.8
  233.8 73.2 reduce-scatter.12
  479.6 45.7 reduce-scatter.10
  528.4 73.3 reduce-scatter.14
